TPU v7x, 32 devices: a whole 2x2x4 slice. The times are simulated.
32 devices in a mesh: groups: 2 (over y), frame: 8 (over z, x), head: 2 (over core).
Axes of the slice: x: 2, y: 2, z: 4, core: 2. Of those that a mesh axis runs over, the one named last changes fastest.
Arguments:
- head_queries: bfloat16 [4096, 1536], P(('groups', 'frame'), 'head'), parts along dimension 0, may hold values from -10 to 10
- head_keys: bfloat16 [4096, 1536], P(('groups', 'frame'), 'head'), parts along dimension 0, may hold values from -10 to 10
- head_values: bfloat16 [4096, 1536], P(('groups', 'frame'), 'head'), parts along dimension 0, may hold values from -18 to 18
- out_weight: bfloat16 [1536, 3072], P('head', 'frame'), may hold values from -0.15625 to 0.15625
- head_class: int32 [12], P('head'), may hold values from 0 to 1, as said below
- block_lists: int32 [12, 16, 4, 2], P('head', ('groups', 'frame')), parts along dimension 1, may hold values from 0 to 3, as said below
- block_counts: int32 [12, 16, 4], P('head', ('groups', 'frame')), parts along dimension 1, may hold values from 1 to 2, as said below
Outputs:
- projected: bfloat16 [4096, 3072], P(('groups', 'frame', 'head')), parts along dimension 0
There are 2 independent parts, one for each index of `groups`. A program takes and returns all parts, laid end to end along the dimension named above; an argument that names none is the same for every part. Nothing has to cross between parts.
Inputs may be any that keep to these rules, and one draw needn't show every extreme that they name: `head_class`: for each j from 0 to 1, exactly half of the heads j * 6 to (j + 1) * 6 - 1 are temporal. block_lists[h, g, b, 0] equals b, and the entries of one list are distinct. `block_counts`: for each head and sequence some query block uses all 2 entries.
All inputs are finite; a program needn't handle non-finite values.
Results may differ from a plain program's by a relative error of at most 0.0062.
Values may be sent and summed in bfloat16 or wider, within the bound.
No kernel may reach another device: no remote copies, remote signals or barrier semaphores. Data moves between devices by JAX's collectives and lax.ppermute only.
A program may use at most 64 MiB of HBM per device.

v0:
```python
import jax
import jax.numpy as jnp
from jax import lax
from jax.sharding import PartitionSpec as P


def dense_head(queries_h, keys_h, values_h, block_ids, counts):
    block_count = block_ids.shape[0]
    listed_most = block_ids.shape[1]
    block_rows = queries_h.shape[0] // block_count
    usable = jnp.arange(listed_most)[None, :] < counts[:, None]
    linked = jnp.any(
        usable[:, :, None] & (block_ids[:, :, None] == jnp.arange(block_count)[None, None, :]),
        axis=1,
    )
    allowed = jnp.repeat(jnp.repeat(linked, block_rows, axis=0), block_rows, axis=1)
    scores = jnp.dot(queries_h, keys_h.T, preferred_element_type=jnp.float32) * queries_h.shape[
        1
    ] ** (-0.5)
    scores = jnp.where(allowed, scores, -jnp.inf)
    row_max = jnp.max(scores, axis=1, keepdims=True)
    weights = jnp.exp(scores - row_max)
    denominator = jnp.sum(weights, axis=1, keepdims=True)
    rounded = weights.astype(jnp.bfloat16)
    result = jnp.dot(rounded, values_h, preferred_element_type=jnp.float32) / denominator
    return result.astype(jnp.bfloat16)


def attend_heads(queries_h, keys_h, values_h, block_ids, counts):

    def single(inputs):
        return dense_head(*inputs)

    stacked = lax.map(
        single,
        (
            queries_h.transpose(1, 0, 2),
            keys_h.transpose(1, 0, 2),
            values_h.transpose(1, 0, 2),
            block_ids,
            counts,
        ),
    )
    return stacked.transpose(1, 0, 2)


def on_device(
    head_queries, head_keys, head_values, out_weight, head_class, block_lists, block_counts
):
    pixels = head_queries.shape[0]
    local_heads = head_class.shape[0]
    half_heads = local_heads // 2
    head_width = head_queries.shape[1] // local_heads
    groups = lax.axis_size("frame")
    head_order = jnp.argsort(head_class, stable=True)
    inverse = jnp.argsort(head_order)
    spatial_ids = head_order[:half_heads]
    temporal_ids = head_order[half_heads:]
    block_ids = block_lists[:, 0]
    counts = block_counts[:, 0]

    def split_heads(tensor, chosen):
        return jnp.take(tensor.reshape(pixels, local_heads, head_width), chosen, axis=1)

    temporal_q = split_heads(head_queries, temporal_ids).reshape(1, pixels, half_heads * head_width)
    temporal_k = split_heads(head_keys, temporal_ids).reshape(1, pixels, half_heads * head_width)
    temporal_v = split_heads(head_values, temporal_ids).reshape(1, pixels, half_heads * head_width)
    arrived = (
        lax.all_to_all(temporal_q, "frame", split_axis=1, concat_axis=0, tiled=True),
        lax.all_to_all(temporal_k, "frame", split_axis=1, concat_axis=0, tiled=True),
        lax.all_to_all(temporal_v, "frame", split_axis=1, concat_axis=0, tiled=True),
    )
    spatial = attend_heads(
        split_heads(head_queries, spatial_ids),
        split_heads(head_keys, spatial_ids),
        split_heads(head_values, spatial_ids),
        block_ids[spatial_ids],
        counts[spatial_ids],
    )
    temporal = attend_heads(
        arrived[0].reshape(pixels, half_heads, head_width),
        arrived[1].reshape(pixels, half_heads, head_width),
        arrived[2].reshape(pixels, half_heads, head_width),
        block_ids[temporal_ids],
        counts[temporal_ids],
    )
    returned = lax.all_to_all(
        temporal.reshape(groups, pixels // groups, half_heads * head_width),
        "frame",
        split_axis=0,
        concat_axis=1,
        tiled=True,
    )
    joined = jnp.concatenate([spatial, returned.reshape(pixels, half_heads, head_width)], axis=1)
    attended = jnp.take(joined, inverse, axis=1).reshape(pixels, local_heads * head_width)
    partial_out = jnp.dot(
        attended,
        lax.all_gather(out_weight, "frame", axis=1, tiled=True),
        preferred_element_type=jnp.float32,
    )
    projected = lax.psum_scatter(
        partial_out.astype(jnp.bfloat16), "head", scatter_dimension=0, tiled=True
    )
    return projected


def solution(mesh):
    placed = (
        P(("groups", "frame"), "head"),
        P(("groups", "frame"), "head"),
        P(("groups", "frame"), "head"),
        P("head", "frame"),
        P("head"),
        P("head", ("groups", "frame"), None, None),
        P("head", ("groups", "frame"), None),
    )
    return jax.shard_map(
        on_device,
        mesh=mesh,
        in_specs=placed,
        out_specs=P(("groups", "frame", "head"), None),
        check_vma=False,
    )
```

profile of v0, /device:TPU:0, one launch (start us, length us, event | category | flops | bytes accessed | tf_op | source)
XLA Modules:
  0.0 125.5 jit_solution(15839549879468988712)
XLA Ops:
  6.5 0.7 all-gather.2.cloned.1.call-update
  7.3 1.6 %sort.34 = (s32[6]{0:T(128)}, s32[6]{0:T(128)S(1)}) sort(s32[6]{0:T(128)} %param.17, s32[6]{0:T(128)S(1)} %iota.30), dimensions={0}, to_apply=%region_0.0 | sort | flops 18 | bytes 96 | tf_op jit(solution)/shard_map/jit(argsort)/sort | solution.py:55
  9.0 1.2 copy.101
  10.4 1.2 copy.103
  11.8 0.6 gather_fusion.5
  13.0 0.6 gather_fusion.8
  13.6 0.6 gather_fusion.9
  14.6 0.6 gather_fusion.7
  15.2 0.6 gather_fusion.10
  16.6 0.6 broadcast.192
  17.2 1.8 %reduce = bf16[256,384]{1,0:T(8,128)(2,1)S(1)} reduce(bf16[256,1,384]{2,1,0:T(2,128)(2,1)S(1)} %bitcast.137, bf16[]{:T(256)} %broadcast.192), dimensions={1}, to_apply=%bitcast.83.reduce_sub_computation | reduce | bytes 393218
  19.0 0.7 reshape.257
  19.7 7.3 %all-to-all-start = ((bf16[8,2,6144]{2,1,0:T(2,128)(2,1)}), bf16[8,2,6144]{2,1,0:T(2,128)(2,1)S(1)}, u32[]{:S(2)}, u32[]{:S(2)}) async-start(bf16[8,2,6144]{2,1,0:T(2,128)(2,1)} %reshape.257), calls=%async_computation | async-start | bytes 393216 | tf_op jit(solution)/shard_map/all_to_all | solution.py:69
  27.6 1.8 %reduce.1 = bf16[256,384]{1,0:T(8,128)(2,1)S(1)} reduce(bf16[256,1,384]{2,1,0:T(2,128)(2,1)S(1)} %bitcast.139, bf16[]{:T(256)} %broadcast.192), dimensions={1}, to_apply=%bitcast.85.reduce_sub_computation | reduce | bytes 393218
  29.5 0.7 reshape.259
  30.2 8.7 %all-to-all-done = bf16[8,2,6144]{2,1,0:T(2,128)(2,1)S(1)} async-done(((bf16[8,2,6144]{2,1,0:T(2,128)(2,1)}), bf16[8,2,6144]{2,1,0:T(2,128)(2,1)S(1)}, u32[]{:S(2)}, u32[]{:S(2)}) %all-to-all-start) | async-done | bytes 196640 | tf_op jit(solution)/shard_map/all_to_all | solution.py:69
  38.9 4.6 %all-to-all-start.1 = ((bf16[8,2,6144]{2,1,0:T(2,128)(2,1)}), bf16[8,2,6144]{2,1,0:T(2,128)(2,1)S(1)}, u32[]{:S(2)}, u32[]{:S(2)}) async-start(bf16[8,2,6144]{2,1,0:T(2,128)(2,1)} %reshape.259), calls=%async_computation.1 | async-start | bytes 393216 | tf_op jit(solution)/shard_map/all_to_all | solution.py:70
  45.5 1.8 %reduce.2 = bf16[256,384]{1,0:T(8,128)(2,1)S(1)} reduce(bf16[256,1,384]{2,1,0:T(2,128)(2,1)S(1)} %bitcast.138, bf16[]{:T(256)} %broadcast.192), dimensions={1}, to_apply=%bitcast.87.reduce_sub_computation | reduce | bytes 393218
  47.3 0.7 reshape.261
  48.1 5.5 %all-to-all-done.1 = bf16[8,2,6144]{2,1,0:T(2,128)(2,1)S(1)} async-done(((bf16[8,2,6144]{2,1,0:T(2,128)(2,1)}), bf16[8,2,6144]{2,1,0:T(2,128)(2,1)S(1)}, u32[]{:S(2)}, u32[]{:S(2)}) %all-to-all-start.1) | async-done | bytes 196640 | tf_op jit(solution)/shard_map/all_to_all | solution.py:70
  53.6 3.4 %all-to-all-start.2 = ((bf16[8,2,6144]{2,1,0:T(2,128)(2,1)}), bf16[8,2,6144]{2,1,0:T(2,128)(2,1)S(1)}, u32[]{:S(2)}, u32[]{:S(2)}) async-start(bf16[8,2,6144]{2,1,0:T(2,128)(2,1)} %reshape.261), calls=%async_computation.2 | async-start | bytes 393216 | tf_op jit(solution)/shard_map/all_to_all | solution.py:71
  57.0 3.0 %while.20 = (s32[]{:T(128)}, bf16[3,256,128]{2,1,0:T(8,128)(2,1)S(1)}, s32[3,4]{1,0:T(4,128)S(1)}, s32[3,4,2]{1,2,0:T(2,128)S(1)}, bf16[3,256,128]{2,1,0:T(8,128...) while((s32[]{:T(128)}, bf16[3,256,128]{2,1,0:T(8,128)(2,1)S(1)}, ...), condition=%wide.region_6.8_spmd, body=%wide.region_2.7_spmd.sunk | while | flops 34078296 | bytes 1191229 | solution.py:34
  61.2 0.9 sort.35
  63.4 7.5 %all-to-all-done.2 = bf16[8,2,6144]{2,1,0:T(2,128)(2,1)S(1)} async-done(((bf16[8,2,6144]{2,1,0:T(2,128)(2,1)}), bf16[8,2,6144]{2,1,0:T(2,128)(2,1)S(1)}, u32[]{:S(2)}, u32[]{:S(2)}) %all-to-all-start.2) | async-done | bytes 196640 | tf_op jit(solution)/shard_map/all_to_all | solution.py:71
  71.5 3.1 %while.21 = (s32[]{:T(128)}, bf16[3,256,128]{2,1,0:T(8,128)(2,1)S(1)}, s32[3,4]{1,0:T(4,128)S(1)}, s32[3,4,2]{1,2,0:T(2,128)S(1)}, bf16[3,256,128]{1,2,0:T(8,128...) while((s32[]{:T(128)}, ...), condition=%wide.region_11.13_spmd, body=%wide.region_7.12_spmd.sunk | while | flops 34078296 | bytes 1191229 | solution.py:34
  74.8 0.8 reshape.144
  75.7 3.4 %all-to-all-start.3 = ((bf16[8,32,384]{2,1,0:T(8,128)(2,1)}), bf16[8,32,384]{2,1,0:T(8,128)(2,1)S(1)}, u32[]{:S(2)}, u32[]{:S(2)}) async-start(bf16[8,32,384]{2,1,0:T(8,128)(2,1)} %reshape.144), calls=%async_computation.3 | async-start | bytes 393216 | tf_op jit(solution)/shard_map/all_to_all | solution.py:87
  79.3 9.9 %all-to-all-done.3 = bf16[8,32,384]{2,1,0:T(8,128)(2,1)S(1)} async-done(((bf16[8,32,384]{2,1,0:T(8,128)(2,1)}), bf16[8,32,384]{2,1,0:T(8,128)(2,1)S(1)}, u32[]{:S(2)}, u32[]{:S(2)}) %all-to-all-start.3) | async-done | bytes 196640 | tf_op jit(solution)/shard_map/all_to_all | solution.py:87
  89.3 0.6 gather_fusion.4
  90.3 14.7 %all-gather.2.cloned.1.call-done = bf16[768,3072]{1,0:T(8,128)(2,1)} async-done(((bf16[768,384]{1,0:T(8,128)(2,1)}), bf16[768,3072]{1,0:T(8,128)(2,1)}) %all-gather.2.cloned.1.call-update) | async-done | bytes 4718608 | tf_op jit(solution)/shard_map/all_gather | solution.py:98
  104.9 4.9 %convolution_convert_fusion = bf16[256,3072]{1,0:T(8,128)(2,1)} fusion(bf16[256,768]{0,1:T(8,128)(2,1)S(1)} %bitcast_select_fusion, bf16[768,3072]{1,0:T(8,128)(2,1)} %all-gather.2.cloned.1.call-done), kind=kOutput, calls=%fused_computation.63 | convolution fusion | flops 1208745984 | bytes 6684672 | tf_op jit(solution)/shard_map/dot_general | solution.py:96
  109.9 8.7 %reduce-scatter.2.cloned.1.call-done = bf16[128,3072]{1,0:T(8,128)(2,1)} async-done(((bf16[256,3072]{1,0:T(8,128)(2,1)}), bf16[128,3072]{1,0:T(8,128)(2,1)}) %reduce-scatter.2.cloned.1.call-update) | async-done | bytes 786448 | tf_op jit(solution)/shard_map/reduce_scatter | solution.py:101
  (117 shorter events, 14.5 us)
Async XLA Ops:
  6.5 7.6 %copy-start = (bf16[256,768]{1,0:T(8,128)(2,1)S(1)}, bf16[256,768]{1,0:T(8,128)(2,1)}, u32[]{:S(2)}) copy-start(bf16[256,768]{1,0:T(8,128)(2,1)} %param.15) | copy-start | bytes 1179652
  6.5 98.4 %all-gather.2.cloned.1.call-start = ((), (), s32[]{:S(2)}) async-start(), calls=%async_computation.5 | async-start | bytes 5308416 | tf_op jit(solution)/shard_map/all_gather | solution.py:98
  14.2 29.4 %copy-start.1 = (s32[6,1,4,2]{0,3,2,1:T(2,128)S(1)}, s32[6,1,4,2]{0,3,2,1:T(2,128)}, u32[]{:S(2)}) copy-start(s32[6,1,4,2]{0,3,2,1:T(2,128)} %param.18) | copy-start | bytes 580
  14.2 30.0 %copy-start.2 = (s32[6,1,4]{0,2,1:T(4,128)S(1)}, s32[6,1,4]{0,2,1:T(4,128)}, u32[]{:S(2)}) copy-start(s32[6,1,4]{0,2,1:T(4,128)} %param.19) | copy-start | bytes 292
  19.7 19.2 %all-to-all-start = ((bf16[8,2,6144]{2,1,0:T(2,128)(2,1)}), bf16[8,2,6144]{2,1,0:T(2,128)(2,1)S(1)}, u32[]{:S(2)}, u32[]{:S(2)}) async-start(bf16[8,2,6144]{2,1,0:T(2,128)(2,1)} %reshape.257), calls=%async_computation | async-start | bytes 393216 | tf_op jit(solution)/shard_map/all_to_all | solution.py:69
  38.9 14.7 %all-to-all-start.1 = ((bf16[8,2,6144]{2,1,0:T(2,128)(2,1)}), bf16[8,2,6144]{2,1,0:T(2,128)(2,1)S(1)}, u32[]{:S(2)}, u32[]{:S(2)}) async-start(bf16[8,2,6144]{2,1,0:T(2,128)(2,1)} %reshape.259), calls=%async_computation.1 | async-start | bytes 393216 | tf_op jit(solution)/shard_map/all_to_all | solution.py:70
  53.6 17.3 %all-to-all-start.2 = ((bf16[8,2,6144]{2,1,0:T(2,128)(2,1)}), bf16[8,2,6144]{2,1,0:T(2,128)(2,1)S(1)}, u32[]{:S(2)}, u32[]{:S(2)}) async-start(bf16[8,2,6144]{2,1,0:T(2,128)(2,1)} %reshape.261), calls=%async_computation.2 | async-start | bytes 393216 | tf_op jit(solution)/shard_map/all_to_all | solution.py:71
  75.7 13.5 %all-to-all-start.3 = ((bf16[8,32,384]{2,1,0:T(8,128)(2,1)}), bf16[8,32,384]{2,1,0:T(8,128)(2,1)S(1)}, u32[]{:S(2)}, u32[]{:S(2)}) async-start(bf16[8,32,384]{2,1,0:T(8,128)(2,1)} %reshape.144), calls=%async_computation.3 | async-start | bytes 393216 | tf_op jit(solution)/shard_map/all_to_all | solution.py:87
  79.1 39.5 %reduce-scatter.2.cloned.1.call-start = ((), (), s32[]{:S(2)}) async-start(), calls=%async_computation.6 | async-start | bytes 2359296 | tf_op jit(solution)/shard_map/reduce_scatter | solution.py:101
Sparse Core Ops, SparseCore 0:
  9.4 95.4 all-gather.1
  110.0 8.5 reduce-scatter.1
where the time goes:
time: 126 us; the launch traced here: 125 us
  waiting for transfers between devices  55.8 us (44%)
  local copies, waits for them, and re-layouts  19.5 us (15%)
  starting transfers between devices  18.7 us (15%)
  between operations  13.7 us (11%)
  other arithmetic  9.56 us (8%)
  matrix products  7.91 us (6%)
    all_gather x1, waiting for transfers between devices, on_device(): lax.all_gather(out_weight, 'frame', axis=1, tiled=True)  14.7 us
    all_to_all x1, waiting for transfers between devices, on_device(): lax.all_to_all(temporal.reshape(groups, pixels // groups, half_heads * he...  9.88 us
    reduce_scatter x1, waiting for transfers between devices, on_device(): lax.psum_scatter(partial_out.astype(jnp.bfloat16), 'head', scatter_dimens...  8.74 us
    all_to_all x1, waiting for transfers between devices, on_device(): lax.all_to_all(temporal_q, 'frame', split_axis=1, concat_axis=0, tiled=True)  8.72 us
    all_to_all x1, waiting for transfers between devices, on_device(): lax.all_to_all(temporal_v, 'frame', split_axis=1, concat_axis=0, tiled=True)  7.5 us
    all_to_all x1, starting transfers between devices, on_device(): lax.all_to_all(temporal_q, 'frame', split_axis=1, concat_axis=0, tiled=True)  7.25 us
    unnamed x17, local copies, waits for them, and re-layouts  5.83 us
    unnamed x3, other arithmetic  5.54 us
  transfers between devices with their start and end apart: 6, of which 6 were waited for; matrix products, arithmetic and copies ran while one was open for 25% of the time, Pallas kernels for 0%

commit v1 on v0

--- a/solution.py
+++ b/solution.py
@@ -2,6 +2,19 @@
 import jax.numpy as jnp
 from jax import lax
 from jax.sharding import PartitionSpec as P
+
+
+def ring_gather(shard, axis, dim):
+    ways = lax.axis_size(axis)
+    up = [(d, (d + 1) % ways) for d in range(ways)]
+    down = [(d, (d - 1) % ways) for d in range(ways)]
+    earlier, later = ([shard], [shard])
+    for _ in range(ways // 2):
+        earlier.append(lax.ppermute(earlier[-1], axis, up))
+    for _ in range((ways - 1) // 2):
+        later.append(lax.ppermute(later[-1], axis, down))
+    line = jnp.concatenate([*earlier[::-1], *later[1:]], axis=dim)
+    return jnp.roll(line, (lax.axis_index(axis) - ways // 2) * shard.shape[dim], axis=dim)
 
 
 def dense_head(queries_h, keys_h, values_h, block_ids, counts):
@@ -94,9 +107,7 @@
     joined = jnp.concatenate([spatial, returned.reshape(pixels, half_heads, head_width)], axis=1)
     attended = jnp.take(joined, inverse, axis=1).reshape(pixels, local_heads * head_width)
     partial_out = jnp.dot(
-        attended,
-        lax.all_gather(out_weight, "frame", axis=1, tiled=True),
-        preferred_element_type=jnp.float32,
+        attended, ring_gather(out_weight, "frame", 1), preferred_element_type=jnp.float32
     )
     projected = lax.psum_scatter(
         partial_out.astype(jnp.bfloat16), "head", scatter_dimension=0, tiled=True

time: 126 us -> 163 us (1.29)
  starting transfers between devices: 18.7 us -> 48.6 us
  waiting for transfers between devices: 55.8 us -> 30.9 us
  local copies, waits for them, and re-layouts: 19.5 us -> 39.5 us
  other arithmetic: 9.56 us -> 17.1 us
  matrix products: 7.91 us -> 11.3 us
    ppermute x0 -> x7, waiting for transfers between devices: none -> 17.5 us  [the longest x3 17.5 us: ring_gather(): later.append(lax.ppermute(later[-1], axis, down))]
    ppermute x0 -> x7, starting transfers between devices: none -> 16.2 us  [the longest x3 10.8 us: ring_gather(): later.append(lax.ppermute(later[-1], axis, down))]
    all_gather x1 -> x0, waiting for transfers between devices: 14.7 us -> none  [on_device(): lax.all_gather(out_weight, 'frame', axis=1, tiled=True)]
    all_to_all x1, starting transfers between devices: 4.62 us -> 14 us  [on_device(): lax.all_to_all(temporal_k, 'frame', split_axis=1, concat_axis=0, tiled=True)]
    all_to_all x1, waiting for transfers between devices: 9.88 us -> 0.65 us  [on_device(): lax.all_to_all(temporal.reshape(groups, pixels // groups, half_heads * he...]
    all_to_all x1, waiting for transfers between devices: 7.5 us -> 0.01 us  [on_device(): lax.all_to_all(temporal_v, 'frame', split_axis=1, concat_axis=0, tiled=True)]
    all_to_all x1, waiting for transfers between devices: 5.54 us -> 0.01 us  [on_device(): lax.all_to_all(temporal_k, 'frame', split_axis=1, concat_axis=0, tiled=True)]
    unnamed x17 -> x42, local copies, waits for them, and re-layouts: 5.83 us -> 11 us
  transfers between devices with their start and end apart: 6 -> 12, of which waited for: 6 -> 5; matrix products, arithmetic and copies ran while one was open for 25% -> 30% of each run, Pallas kernels for 0% -> 0%
where the time goes in v1:
time: 163 us; the launch traced here: 161 us
  starting transfers between devices  48.6 us (30%)
  local copies, waits for them, and re-layouts  39.5 us (24%)
  waiting for transfers between devices  30.9 us (19%)
  other arithmetic  17.1 us (10%)
  between operations  13.8 us (8%)
  matrix products  11.3 us (7%)
    ppermute x3, waiting for transfers between devices, ring_gather(): later.append(lax.ppermute(later[-1], axis, down))  17.5 us
    all_to_all x1, starting transfers between devices, on_device(): lax.all_to_all(temporal_k, 'frame', split_axis=1, concat_axis=0, tiled=True)  14 us
    unnamed x42, local copies, waits for them, and re-layouts  11 us
    ppermute x3, starting transfers between devices, ring_gather(): later.append(lax.ppermute(later[-1], axis, down))  10.8 us
    reduce_scatter x1, waiting for transfers between devices, on_device(): lax.psum_scatter(partial_out.astype(jnp.bfloat16), 'head', scatter_dimens...  8.8 us
    all_to_all x1, starting transfers between devices, on_device(): lax.all_to_all(temporal_q, 'frame', split_axis=1, concat_axis=0, tiled=True)  7.25 us
    all_to_all x1, starting transfers between devices, on_device(): lax.all_to_all(temporal_v, 'frame', split_axis=1, concat_axis=0, tiled=True)  6.69 us
    dot_general x6, matrix products, dense_head(): jnp.dot(rounded, values_h, preferred_element_type=jnp.float32) / denominator  6.54 us
  transfers between devices with their start and end apart: 12, of which 5 were waited for; matrix products, arithmetic and copies ran while one was open for 30% of the time, Pallas kernels for 0%

profile of v1, /device:TPU:0, one launch (start us, length us, event | category | flops | bytes accessed | tf_op | source)
XLA Modules:
  0.0 161.5 jit_solution(16343145466773676660)
XLA Ops:
  6.5 1.7 %sort.34 = (s32[6]{0:T(128)}, s32[6]{0:T(128)S(1)}) sort(s32[6]{0:T(128)} %param.17, s32[6]{0:T(128)S(1)} %iota.30), dimensions={0}, to_apply=%region_0.0 | sort | flops 18 | bytes 96 | tf_op jit(solution)/shard_map/jit(argsort)/sort | solution.py:68
  8.3 1.2 copy.101
  9.7 1.2 copy.103
  13.5 1.2 copy.105
  18.1 1.8 %reduce = bf16[256,384]{1,0:T(8,128)(2,1)S(1)} reduce(bf16[256,1,384]{2,1,0:T(2,128)(2,1)S(1)} %bitcast.136, bf16[]{:T(256)} %broadcast.192), dimensions={1}, to_apply=%bitcast.83.reduce_sub_computation | reduce | bytes 393218
  20.7 7.3 %all-to-all-start = ((bf16[8,2,6144]{2,1,0:T(2,128)(2,1)}), bf16[8,2,6144]{2,1,0:T(2,128)(2,1)S(1)}, u32[]{:S(2)}, u32[]{:S(2)}) async-start(bf16[8,2,6144]{2,1,0:T(2,128)(2,1)} %reshape.257), calls=%async_computation | async-start | bytes 393216 | tf_op jit(solution)/shard_map/all_to_all | solution.py:82
  28.0 2.0 %collective-permute-start = (bf16[768,384]{1,0:T(8,128)(2,1)S(1)}, bf16[768,384]{1,0:T(8,128)(2,1)S(1)}, u32[]{:S(2)}, u32[]{:S(2)}) collective-permute-start(bf16[768,384]{1,0:T(8,128)(2,1)S(1)} %copy-done), channel_id=1, source_target_pairs={{0,2},{2,4},{4,6},{6,8},{8,10},{10,12},{12,14},{14,0},{1,3},{3,5},... | collective-permute-start | bytes 1769480 | tf_op jit(solution)/shard_map/ppermute | solution.py:13
  30.6 1.8 %reduce.1 = bf16[256,384]{1,0:T(8,128)(2,1)S(1)} reduce(bf16[256,1,384]{2,1,0:T(2,128)(2,1)S(1)} %bitcast.138, bf16[]{:T(256)} %broadcast.192), dimensions={1}, to_apply=%bitcast.85.reduce_sub_computation | reduce | bytes 393218
  33.2 3.9 %all-to-all-done = bf16[8,2,6144]{2,1,0:T(2,128)(2,1)S(1)} async-done(((bf16[8,2,6144]{2,1,0:T(2,128)(2,1)}), bf16[8,2,6144]{2,1,0:T(2,128)(2,1)S(1)}, u32[]{:S(2)}, u32[]{:S(2)}) %all-to-all-start) | async-done | bytes 196640 | tf_op jit(solution)/shard_map/all_to_all | solution.py:82
  37.1 14.0 %all-to-all-start.1 = ((bf16[8,2,6144]{2,1,0:T(2,128)(2,1)}), bf16[8,2,6144]{2,1,0:T(2,128)(2,1)S(1)}, u32[]{:S(2)}, u32[]{:S(2)}) async-start(bf16[8,2,6144]{2,1,0:T(2,128)(2,1)} %reshape.259), calls=%async_computation.1 | async-start | bytes 393216 | tf_op jit(solution)/shard_map/all_to_all | solution.py:83
  51.1 4.7 %collective-permute-start.4 = (bf16[768,384]{1,0:T(8,128)(2,1)S(1)}, bf16[768,384]{1,0:T(8,128)(2,1)S(1)}, u32[]{:S(2)}, u32[]{:S(2)}) collective-permute-start(bf16[768,384]{1,0:T(8,128)(2,1)S(1)} %copy-done), channel_id=1, source_target_pairs={{0,14},{2,0},{4,2},{6,4},{8,6},{10,8},{12,10},{14,12},{1,15},{3,1}... | collective-permute-start | bytes 1769480 | tf_op jit(solution)/shard_map/ppermute | solution.py:15
  58.3 1.8 %reduce.2 = bf16[256,384]{1,0:T(8,128)(2,1)S(1)} reduce(bf16[256,1,384]{2,1,0:T(2,128)(2,1)S(1)} %bitcast.137, bf16[]{:T(256)} %broadcast.192), dimensions={1}, to_apply=%bitcast.87.reduce_sub_computation | reduce | bytes 393218
  60.9 6.7 %all-to-all-start.2 = ((bf16[8,2,6144]{2,1,0:T(2,128)(2,1)}), bf16[8,2,6144]{2,1,0:T(2,128)(2,1)S(1)}, u32[]{:S(2)}, u32[]{:S(2)}) async-start(bf16[8,2,6144]{2,1,0:T(2,128)(2,1)} %reshape.261), calls=%async_computation.2 | async-start | bytes 393216 | tf_op jit(solution)/shard_map/all_to_all | solution.py:84
  67.6 11.3 %while.20 = (s32[]{:T(128)}, bf16[3,256,128]{2,1,0:T(8,128)(2,1)S(1)}, s32[3,4]{1,0:T(4,128)}, s32[3,4,2]{1,2,0:T(2,128)S(1)}, bf16[3,256,128]{2,1,0:T(8,128)(2,...) while((s32[]{:T(128)}, bf16[3,256,128]{2,1,0:T(8,128)(2,1)S(1)}, ...), condition=%wide.region_6.8_spmd, body=%wide.region_2.7_spmd.sunk | while | flops 34078296 | bytes 1191229 | solution.py:47
  78.9 1.4 gather_fusion.3
  80.3 1.3 gather_fusion.2
  81.6 1.6 sort.35
  86.1 2.1 %collective-permute-start.2 = (bf16[768,384]{1,0:T(8,128)(2,1)S(1)}, bf16[768,384]{1,0:T(8,128)(2,1)S(1)}, u32[]{:S(2)}, u32[]{:S(2)}) collective-permute-start(bf16[768,384]{1,0:T(8,128)(2,1)S(1)} %collective-permute-done.1), channel_id=1, source_target_pairs={{0,2},{2,4},{4,6},{6,8},{8,10},{10,12},{12,14},{14,0},{1,3},{3,5},... | collective-permute-start | bytes 1769480 | tf_op jit(solution)/shard_map/ppermute | solution.py:13
  88.2 7.7 %while.21 = (s32[]{:T(128)}, bf16[3,256,128]{2,1,0:T(8,128)(2,1)S(1)}, s32[3,4]{1,0:T(4,128)}, s32[3,4,2]{1,2,0:T(2,128)S(1)}, bf16[3,256,128]{1,2,0:T(8,128)(2,...) while((s32[]{:T(128)}, bf16[3,256,128]{2,1,0:T(8,128)(2,1)S(1)}, ...), condition=%wide.region_11.13_spmd, body=%wide.region_7.12_spmd.sunk | while | flops 34078296 | bytes 1191229 | solution.py:47
  96.9 4.5 %all-to-all-start.3 = ((bf16[8,32,384]{2,1,0:T(8,128)(2,1)}), bf16[8,32,384]{2,1,0:T(8,128)(2,1)}, u32[]{:S(2)}, u32[]{:S(2)}) async-start(bf16[8,32,384]{2,1,0:T(8,128)(2,1)} %reshape.144), calls=%async_computation.3 | async-start | bytes 393216 | tf_op jit(solution)/shard_map/all_to_all | solution.py:100
  102.7 4.7 %collective-permute-start.5 = (bf16[768,384]{1,0:T(8,128)(2,1)S(1)}, bf16[768,384]{1,0:T(8,128)(2,1)S(1)}, u32[]{:S(2)}, u32[]{:S(2)}) collective-permute-start(bf16[768,384]{1,0:T(8,128)(2,1)S(1)} %collective-permute-done.4), channel_id=1, source_target_pairs={{0,14},{2,0},{4,2},{6,4},{8,6},{10,8},{12,10},{14,12},{1,15},{3,1}... | collective-permute-start | bytes 1769480 | tf_op jit(solution)/shard_map/ppermute | solution.py:15
  107.4 1.3 collective-permute-start.3
  109.4 1.7 %reshape.145 = bf16[256,3,128]{2,1,0:T(4,128)(2,1)} reshape(bf16[8,32,384]{2,1,0:T(8,128)(2,1)} %all-to-all-done.3) | data formatting | bytes 393216 | tf_op jit(solution)/shard_map/reshape | solution.py:107
  112.1 1.7 %pad_maximum_fusion = bf16[256,6,128]{2,0,1:T(8,128)(2,1)} fusion(bf16[256,3,128]{2,0,1:T(8,128)(2,1)S(1)} %copy.125, bf16[256,3,128]{2,0,1:T(8,128)(2,1)} %bitcast.142), kind=kLoop, calls=%fused_computation.66 | loop fusion | flops 196608 | bytes 786432 | tf_op jit(solution)/shard_map/concatenate | solution.py:107
  113.8 2.3 %gather_fusion.4 = bf16[6,256,128]{2,1,0:T(8,128)(2,1)} fusion(bf16[256,6,128]{2,0,1:T(8,128)(2,1)} %pad_maximum_fusion, s32[1024]{0:T(1024)S(1)} %pad_clamp_fusion), kind=kCustom, calls=%fused_computation.10 | custom fusion | bytes 786456 | tf_op jit(solution)/shard_map/jit(_take)/gather | solution.py:108
  116.1 1.9 %copy.126 = bf16[256,6,128]{0,2,1:T(8,128)(2,1)} copy(bf16[256,6,128]{2,0,1:T(8,128)(2,1)} %bitcast.129) | data formatting | bytes 786432 | tf_op jit(solution)/shard_map/jit(_take)/gather | solution.py:108
  119.2 6.7 %collective-permute-done.5 = bf16[768,384]{1,0:T(8,128)(2,1)S(1)} collective-permute-done((bf16[768,384]{1,0:T(8,128)(2,1)S(1)}, bf16[768,384]{1,0:T(8,128)(2,1)S(1)}, u32[]{:S(2)}, u32[]{:S(2)}) %collective-permute-start.5) | collective-permute-done | bytes 589856 | tf_op jit(solution)/shard_map/ppermute | solution.py:15
  125.9 1.4 collective-permute-start.6
  129.4 10.8 %collective-permute-done.6 = bf16[768,384]{1,0:T(8,128)(2,1)S(1)} collective-permute-done((bf16[768,384]{1,0:T(8,128)(2,1)S(1)}, bf16[768,384]{1,0:T(8,128)(2,1)S(1)}, u32[]{:S(2)}, u32[]{:S(2)}) %collective-permute-start.6) | collective-permute-done | bytes 589856 | tf_op jit(solution)/shard_map/ppermute | solution.py:15
  140.3 1.2 constant_dynamic-update-slice_fusion.7
  142.5 3.2 %fusion.42 = bf16[256,3072]{1,0:T(8,128)(2,1)} fusion(bf16[256,768]{0,1:T(8,128)(2,1)S(1)} %bitcast_select_fusion, bf16[768,6144]{1,0:T(8,128)(2,1)S(1)} %constant_dynamic-update-slice_fusion, s32[]{:T(128)S(6)} %select_n.50), kind=kOutput, calls=%fused_computation.65 | convolution fusion | flops 1208745984 | bytes 6684676 | tf_op jit(solution)/shard_map/dot_general | solution.py:109
  145.8 8.8 %reduce-scatter.2.cloned.1.call-done = bf16[128,3072]{1,0:T(8,128)(2,1)} async-done(((bf16[256,3072]{1,0:T(8,128)(2,1)}), bf16[128,3072]{1,0:T(8,128)(2,1)}) %reduce-scatter.2.cloned.1.call-update) | async-done | bytes 786448 | tf_op jit(solution)/shard_map/reduce_scatter | solution.py:112
  (154 shorter events, 41.6 us)
Async XLA Ops:
  6.5 21.4 %copy-start = (bf16[768,384]{1,0:T(8,128)(2,1)S(1)}, bf16[768,384]{1,0:T(8,128)(2,1)}, u32[]{:S(2)}) copy-start(bf16[768,384]{1,0:T(8,128)(2,1)} %param.16) | copy-start | bytes 1769476
  6.5 49.3 %copy-start.4 = (s32[6,1,4,2]{0,3,2,1:T(2,128)S(1)}, s32[6,1,4,2]{0,3,2,1:T(2,128)}, u32[]{:S(2)}) copy-start(s32[6,1,4,2]{0,3,2,1:T(2,128)} %param.18) | copy-start | bytes 580
  6.5 50.0 %copy-start.5 = (s32[6,1,4]{0,2,1:T(4,128)S(1)}, s32[6,1,4]{0,2,1:T(4,128)}, u32[]{:S(2)}) copy-start(s32[6,1,4]{0,2,1:T(4,128)} %param.19) | copy-start | bytes 292
  8.2 7.9 %copy-start.6 = (s32[6]{0:T(128)}, s32[6]{0:T(128)S(1)}, u32[]{:S(2)}) copy-start(s32[6]{0:T(128)S(1)} %get-tuple-element.82) | copy-start | bytes 76
  12.3 3.8 %copy-start.3 = (s32[1024]{0:T(1024)}, s32[1024]{0:T(1024)S(1)}, u32[]{:S(2)}) copy-start(s32[1024]{0:T(1024)S(1)} %pad_clamp_fusion.1) | copy-start | bytes 12292
  20.7 16.4 %all-to-all-start = ((bf16[8,2,6144]{2,1,0:T(2,128)(2,1)}), bf16[8,2,6144]{2,1,0:T(2,128)(2,1)S(1)}, u32[]{:S(2)}, u32[]{:S(2)}) async-start(bf16[8,2,6144]{2,1,0:T(2,128)(2,1)} %reshape.257), calls=%async_computation | async-start | bytes 393216 | tf_op jit(solution)/shard_map/all_to_all | solution.py:82
  28.0 32.9 %collective-permute-start = (bf16[768,384]{1,0:T(8,128)(2,1)S(1)}, bf16[768,384]{1,0:T(8,128)(2,1)S(1)}, u32[]{:S(2)}, u32[]{:S(2)}) collective-permute-start(bf16[768,384]{1,0:T(8,128)(2,1)S(1)} %copy-done), channel_id=1, source_target_pairs={{0,2},{2,4},{4,6},{6,8},{8,10},{10,12},{12,14},{14,0},{1,3},{3,5},... | collective-permute-start | bytes 1769480 | tf_op jit(solution)/shard_map/ppermute | solution.py:13
  37.1 23.8 %all-to-all-start.1 = ((bf16[8,2,6144]{2,1,0:T(2,128)(2,1)}), bf16[8,2,6144]{2,1,0:T(2,128)(2,1)S(1)}, u32[]{:S(2)}, u32[]{:S(2)}) async-start(bf16[8,2,6144]{2,1,0:T(2,128)(2,1)} %reshape.259), calls=%async_computation.1 | async-start | bytes 393216 | tf_op jit(solution)/shard_map/all_to_all | solution.py:83
  51.1 51.6 %collective-permute-start.4 = (bf16[768,384]{1,0:T(8,128)(2,1)S(1)}, bf16[768,384]{1,0:T(8,128)(2,1)S(1)}, u32[]{:S(2)}, u32[]{:S(2)}) collective-permute-start(bf16[768,384]{1,0:T(8,128)(2,1)S(1)} %copy-done), channel_id=1, source_target_pairs={{0,14},{2,0},{4,2},{6,4},{8,6},{10,8},{12,10},{14,12},{1,15},{3,1}... | collective-permute-start | bytes 1769480 | tf_op jit(solution)/shard_map/ppermute | solution.py:15
  55.9 11.7 %copy-start.2 = (s32[6,4,2]{1,2,0:T(2,128)}, s32[6,4,2]{1,2,0:T(2,128)S(1)}, u32[]{:S(2)}) copy-start(s32[6,4,2]{1,2,0:T(2,128)S(1)} %copy.100) | copy-start | bytes 580
  60.9 25.2 %collective-permute-start.1 = (bf16[768,384]{1,0:T(8,128)(2,1)S(1)}, bf16[768,384]{1,0:T(8,128)(2,1)S(1)}, u32[]{:S(2)}, u32[]{:S(2)}) collective-permute-start(bf16[768,384]{1,0:T(8,128)(2,1)S(1)} %collective-permute-done), channel_id=1, source_target_pairs={{0,2},{2,4},{4,6},{6,8},{8,10},{10,12},{12,14},{14,0},{1,3},{3,5},... | collective-permute-start | bytes 1769480 | tf_op jit(solution)/shard_map/ppermute | solution.py:13
  60.9 24.0 %all-to-all-start.2 = ((bf16[8,2,6144]{2,1,0:T(2,128)(2,1)}), bf16[8,2,6144]{2,1,0:T(2,128)(2,1)S(1)}, u32[]{:S(2)}, u32[]{:S(2)}) async-start(bf16[8,2,6144]{2,1,0:T(2,128)(2,1)} %reshape.261), calls=%async_computation.2 | async-start | bytes 393216 | tf_op jit(solution)/shard_map/all_to_all | solution.py:84
  78.9 5.0 %copy-start.1 = (bf16[3,256,128]{2,1,0:T(8,128)(2,1)}, bf16[3,256,128]{2,1,0:T(8,128)(2,1)S(1)}, u32[]{:S(2)}) copy-start(bf16[3,256,128]{2,1,0:T(8,128)(2,1)S(1)} %get-tuple-element.84) | copy-start | bytes 589828
  83.2 5.0 %copy-start.7 = (s32[6]{0:T(128)}, s32[6]{0:T(128)S(1)}, u32[]{:S(2)}) copy-start(s32[6]{0:T(128)S(1)} %get-tuple-element.83) | copy-start | bytes 76
  86.1 21.3 %collective-permute-start.2 = (bf16[768,384]{1,0:T(8,128)(2,1)S(1)}, bf16[768,384]{1,0:T(8,128)(2,1)S(1)}, u32[]{:S(2)}, u32[]{:S(2)}) collective-permute-start(bf16[768,384]{1,0:T(8,128)(2,1)S(1)} %collective-permute-done.1), channel_id=1, source_target_pairs={{0,2},{2,4},{4,6},{6,8},{8,10},{10,12},{12,14},{14,0},{1,3},{3,5},... | collective-permute-start | bytes 1769480 | tf_op jit(solution)/shard_map/ppermute | solution.py:13
  96.9 12.5 %all-to-all-start.3 = ((bf16[8,32,384]{2,1,0:T(8,128)(2,1)}), bf16[8,32,384]{2,1,0:T(8,128)(2,1)}, u32[]{:S(2)}, u32[]{:S(2)}) async-start(bf16[8,32,384]{2,1,0:T(8,128)(2,1)} %reshape.144), calls=%async_computation.3 | async-start | bytes 393216 | tf_op jit(solution)/shard_map/all_to_all | solution.py:100
  101.4 53.2 %reduce-scatter.2.cloned.1.call-start = ((), (), s32[]{:S(2)}) async-start(), calls=%async_computation.5 | async-start | bytes 2359296 | tf_op jit(solution)/shard_map/reduce_scatter | solution.py:112
  102.7 23.2 %collective-permute-start.5 = (bf16[768,384]{1,0:T(8,128)(2,1)S(1)}, bf16[768,384]{1,0:T(8,128)(2,1)S(1)}, u32[]{:S(2)}, u32[]{:S(2)}) collective-permute-start(bf16[768,384]{1,0:T(8,128)(2,1)S(1)} %collective-permute-done.4), channel_id=1, source_target_pairs={{0,14},{2,0},{4,2},{6,4},{8,6},{10,8},{12,10},{14,12},{1,15},{3,1}... | collective-permute-start | bytes 1769480 | tf_op jit(solution)/shard_map/ppermute | solution.py:15
  107.4 19.9 %collective-permute-start.3 = (bf16[768,384]{1,0:T(8,128)(2,1)S(1)}, bf16[768,384]{1,0:T(8,128)(2,1)}, u32[]{:S(2)}, u32[]{:S(2)}) collective-permute-start(bf16[768,384]{1,0:T(8,128)(2,1)S(1)} %collective-permute-done.2), channel_id=1, source_target_pairs={{0,2},{2,4},{4,6},{6,8},{8,10},{10,12},{12,14},{14,0},{1,3},{3,5},... | collective-permute-start | bytes 1769480 | tf_op jit(solution)/shard_map/ppermute | solution.py:13
  125.9 14.3 %collective-permute-start.6 = (bf16[768,384]{1,0:T(8,128)(2,1)S(1)}, bf16[768,384]{1,0:T(8,128)(2,1)S(1)}, u32[]{:S(2)}, u32[]{:S(2)}) collective-permute-start(bf16[768,384]{1,0:T(8,128)(2,1)S(1)} %collective-permute-done.5), channel_id=1, source_target_pairs={{0,14},{2,0},{4,2},{6,4},{8,6},{10,8},{12,10},{14,12},{1,15},{3,1}... | collective-permute-start | bytes 1769480 | tf_op jit(solution)/shard_map/ppermute | solution.py:15
Sparse Core Ops, SparseCore 0:
  145.9 8.6 reduce-scatter.1
